TPU v7x, 32 devices: a whole 2x2x4 slice. The times are simulated.
32 devices in a mesh: group: 2 (over y), dev: 8 (over z, x), tp: 2 (over core).
Axes of the slice: x: 2, y: 2, z: 4, core: 2. Of those that a mesh axis runs over, the one named last changes fastest.
Arguments:
- prompt_activations: bfloat16 [4096, 8192], P(('group', 'dev')), parts along dimension 0, may hold values from -6 to 6
- key_matrix: bfloat16 [8192, 512], P('dev', 'tp'), may hold values from -0.0625 to 0.0625
- value_matrix: bfloat16 [8192, 512], P('dev', 'tp'), may hold values from -0.0625 to 0.0625
- adapter_down_keyvalue: bfloat16 [8192, 128], P('dev'), may hold values from -0.0625 to 0.0625
- adapter_up_key: bfloat16 [64, 512], P(None, 'tp'), may hold values from -1.5 to 1.5
- adapter_up_value: bfloat16 [64, 512], P(None, 'tp'), may hold values from -1.5 to 1.5
- request_adapter: int32 [16], P('group'), parts along dimension 0, may hold values from 0 to 3
- page_request: int32 [1024, 1], P('group'), parts along dimension 0, may hold values from 0 to 7; in each aligned block of 64 rows (0 to 63, 64 to 127, ...) at most 8 rows name the same one
- context_tokens: int32 [16], P('group'), parts along dimension 0, may hold values from 64 to 256
- step_query: bfloat16 [16, 4096], P(('group', 'dev'), 'tp'), parts along dimension 0, may hold values from -256 to 256
- step_key: bfloat16 [16, 512], P(('group', 'dev'), 'tp'), parts along dimension 0, may hold values from -6 to 6
- step_value: bfloat16 [16, 512], P(('group', 'dev'), 'tp'), parts along dimension 0, may hold values from -6 to 6
- stored_keys: bfloat16 [16, 256, 512], P(('group', 'dev'), None, 'tp'), parts along dimension 0, may hold values from -6 to 6
- stored_values: bfloat16 [16, 256, 512], P(('group', 'dev'), None, 'tp'), parts along dimension 0, may hold values from -6 to 6
- output_matrix: bfloat16 [4096, 8192], P('tp', 'dev'), may hold values from -0.09375 to 0.09375
- adapter_down_output: bfloat16 [4096, 64], P('tp'), may hold values from -0.09375 to 0.09375
- adapter_up_output: bfloat16 [64, 8192], P(None, 'dev'), may hold values from -1.5 to 1.5
Outputs:
- attended: bfloat16 [16, 8192], P('group', 'dev'), parts along dimension 0
There are 2 independent parts, one for each index of `group`. A program takes and returns all parts, laid end to end along the dimension named above; an argument that names none is the same for every part. Nothing has to cross between parts.
Inputs may be any that keep to these rules, and one draw needn't show every extreme that they name: `page_request`: among the pages of one device's prompt block (aligned blocks of 64 pages), no request owns more than 8; every request owns at least one page.
All inputs are finite; a program needn't handle non-finite values.
Results may differ from a plain program's by a relative error of at most 0.0086.
Values may be sent and summed in bfloat16 or wider, within the bound.
A program may use at most 64 MiB of HBM per device.

v0:
```python
import jax
import jax.numpy as jnp
from jax import lax
from jax.sharding import PartitionSpec as P

HEADS = 32
KV_HEADS = 4
HEAD = 128
LOW_RANK = 16
ADAPTER_COUNT = 4
PAGE = 4
adapter_scale = 1.0
rope_base = 500000.0


def rotate(key_rows, positions):
    row_count = key_rows.shape[0]
    blocks = key_rows.reshape(row_count, -1, HEAD)
    half_size = HEAD // 2
    exponent = jnp.arange(half_size, dtype=jnp.float32) * (2.0 / HEAD)
    frequency = jnp.exp(-jnp.log(jnp.float32(rope_base)) * exponent)
    angles = positions.astype(jnp.float32)[:, None] * frequency[None, :]
    cosine = jnp.cos(angles)[:, None, :]
    sine_part = jnp.sin(angles)[:, None, :]
    first_half = blocks[..., :half_size]
    second_half = blocks[..., half_size:]
    turned = jnp.concatenate(
        [
            first_half * cosine - second_half * sine_part,
            second_half * cosine + first_half * sine_part,
        ],
        axis=-1,
    )
    return turned.reshape(row_count, -1)


def owner_ranks(owners, row_total):
    onehot = (owners[:, None] == jnp.arange(row_total, dtype=jnp.int32)[None, :]).astype(jnp.int32)
    before = jnp.cumsum(onehot, axis=0) - onehot
    rank = jnp.sum(before * onehot, axis=1)
    return (onehot, rank)


def mask_columns(narrowed, adapter_list):
    column = jnp.arange(narrowed.shape[1], dtype=jnp.int32)
    owner = column % (ADAPTER_COUNT * LOW_RANK) // LOW_RANK
    return jnp.where(owner[None, :] == adapter_list[:, None], narrowed, jnp.zeros_like(narrowed))


def selected_narrow(activation_rows, adapter_down, adapter_list):
    narrowed = jnp.dot(activation_rows, adapter_down, preferred_element_type=jnp.float32)
    return mask_columns(narrowed, adapter_list)


def widened(selected_rows, up_key, up_value):
    split_at = ADAPTER_COUNT * LOW_RANK
    highest = lax.Precision.HIGHEST
    key_portion = jnp.dot(
        selected_rows[:, :split_at], up_key.astype(jnp.float32), precision=highest
    )
    value_portion = jnp.dot(
        selected_rows[:, split_at:], up_value.astype(jnp.float32), precision=highest
    )
    return (adapter_scale * key_portion, adapter_scale * value_portion)


def attend_local(
    query,
    old_keys,
    old_values,
    old_length,
    fresh_keys,
    fresh_values,
    fresh_valid,
    last_key,
    last_value,
):
    group_size = HEADS // KV_HEADS
    query_heads = query.reshape(-1, group_size, HEAD)
    kv_local = query_heads.shape[0]
    scale_factor = HEAD ** (-0.5)

    def score_of(key_rows):
        shaped = key_rows.reshape(key_rows.shape[0], kv_local, HEAD)
        return (
            jnp.einsum("kgd,lkd->kgl", query_heads, shaped, preferred_element_type=jnp.float32)
            * scale_factor
        )

    def mix_with(probs, value_rows):
        shaped = value_rows.reshape(value_rows.shape[0], kv_local, HEAD)
        return jnp.einsum("kgl,lkd->kgd", probs, shaped, preferred_element_type=jnp.float32)

    old_valid = jnp.arange(old_keys.shape[0], dtype=jnp.int32) < old_length
    old_scores = jnp.where(old_valid[None, None, :], score_of(old_keys), -1e30)
    fresh_scores = jnp.where(fresh_valid[None, None, :], score_of(fresh_keys), -1e30)
    last_score = score_of(last_key[None, :])
    top = jnp.maximum(
        jnp.maximum(
            jnp.max(old_scores, axis=-1, keepdims=True),
            jnp.max(fresh_scores, axis=-1, keepdims=True),
        ),
        last_score,
    )
    old_weights = jnp.exp(old_scores - top)
    fresh_weights = jnp.exp(fresh_scores - top)
    last_weight = jnp.exp(last_score - top)
    total = (
        jnp.sum(old_weights, axis=-1, keepdims=True)
        + jnp.sum(fresh_weights, axis=-1, keepdims=True)
        + last_weight
    )
    output = mix_with((old_weights / total).astype(jnp.bfloat16), old_values)
    output = output + mix_with((fresh_weights / total).astype(jnp.bfloat16), fresh_values)
    output = output + mix_with((last_weight / total).astype(jnp.bfloat16), last_value[None, :])
    return output.reshape(-1).astype(jnp.bfloat16)


def per_device(
    prompt_activations,
    key_matrix,
    value_matrix,
    adapter_down_keyvalue,
    adapter_up_key,
    adapter_up_value,
    request_adapter,
    page_request,
    context_tokens,
    step_query,
    step_key,
    step_value,
    stored_keys,
    stored_values,
    output_matrix,
    adapter_down_output,
    adapter_up_output,
):
    devices = lax.axis_size("dev")
    device = lax.axis_index("dev")
    tok_count = prompt_activations.shape[0]
    pages_here = tok_count // PAGE
    capacity = max(2, (pages_here + devices - 1) // devices)
    row_total = request_adapter.shape[0]
    owners = page_request[:, 0]
    onehot, rank = owner_ranks(owners, row_total)
    first_page = device * pages_here
    my_owners = lax.dynamic_slice_in_dim(owners, first_page, pages_here, 0)
    my_rank = lax.dynamic_slice_in_dim(rank, first_page, pages_here, 0)
    tokens = jnp.arange(tok_count, dtype=jnp.int32)
    token_page = tokens // PAGE
    token_owner = jnp.take(my_owners, token_page)
    position = (
        jnp.take(context_tokens, token_owner) + jnp.take(my_rank, token_page) * PAGE + tokens % PAGE
    )
    adapter_list = jnp.take(request_adapter, token_owner)
    key_width = key_matrix.shape[1]

    def add_rows(portion):
        return jnp.dot(prompt_activations, portion, preferred_element_type=jnp.float32)

    key_raw = add_rows(lax.all_gather(key_matrix, "dev", axis=0, tiled=True))
    value_raw = add_rows(lax.all_gather(value_matrix, "dev", axis=0, tiled=True))
    down_complete = lax.all_gather(adapter_down_keyvalue, "dev", axis=0, tiled=True)
    narrowed = jnp.dot(prompt_activations, down_complete, preferred_element_type=jnp.float32)
    selected_rows = mask_columns(narrowed, adapter_list)
    key_delta, value_delta = widened(selected_rows, adapter_up_key, adapter_up_value)
    key_rows = rotate(key_raw + key_delta, position).astype(jnp.bfloat16)
    value_rows = (value_raw + value_delta).astype(jnp.bfloat16)
    joined_rows = jnp.concatenate([key_rows, value_rows], axis=1)
    local_hot = (my_owners[:, None] == jnp.arange(row_total, dtype=jnp.int32)[None, :]).astype(
        jnp.int32
    )
    local_before = jnp.cumsum(local_hot, axis=0) - local_hot
    local_slot = jnp.sum(local_before * local_hot, axis=1)
    peer_slots = capacity * PAGE
    target = token_owner * peer_slots + jnp.take(local_slot, token_page) * PAGE + tokens % PAGE
    outgoing = (
        jnp.zeros((devices * peer_slots, 2 * key_width), jnp.bfloat16).at[target].set(joined_rows)
    )
    outgoing = outgoing.reshape(devices, peer_slots, 2 * key_width)
    incoming = lax.all_to_all(outgoing, "dev", split_axis=0, concat_axis=0, tiled=True)
    fresh_keys = incoming[:, :, :key_width].reshape(-1, key_width)
    fresh_values = incoming[:, :, key_width:].reshape(-1, key_width)
    my_column = jnp.take(onehot, device, axis=1)
    count_from = jnp.sum(my_column.reshape(devices, pages_here), axis=1)
    slot_page = jnp.arange(peer_slots, dtype=jnp.int32) // PAGE
    fresh_valid = (slot_page[None, :] < count_from[:, None]).reshape(-1)
    mixed_local = attend_local(
        step_query[0],
        stored_keys[0],
        stored_values[0],
        jnp.take(context_tokens, device),
        fresh_keys,
        fresh_values,
        fresh_valid,
        step_key[0],
        step_value[0],
    ).reshape(1, -1)
    portion = lax.all_gather(mixed_local, "dev", axis=0, tiled=True)
    plain_result = jnp.dot(portion, output_matrix, preferred_element_type=jnp.float32)
    selected_output = selected_narrow(portion, adapter_down_output, request_adapter)
    partial_output = plain_result + adapter_scale * jnp.dot(
        selected_output, adapter_up_output.astype(jnp.float32), precision=lax.Precision.HIGHEST
    )
    return lax.psum(partial_output, "tp").astype(jnp.bfloat16)


def solution(mesh):
    return jax.shard_map(
        per_device,
        mesh=mesh,
        in_specs=(
            P(("group", "dev"), None),
            P("dev", "tp"),
            P("dev", "tp"),
            P("dev", None),
            P(None, "tp"),
            P(None, "tp"),
            P("group"),
            P("group", None),
            P("group"),
            P(("group", "dev"), "tp"),
            P(("group", "dev"), "tp"),
            P(("group", "dev"), "tp"),
            P(("group", "dev"), None, "tp"),
            P(("group", "dev"), None, "tp"),
            P("tp", "dev"),
            P("tp", None),
            P(None, "dev"),
        ),
        out_specs=P("group", "dev"),
        check_vma=False,
    )
```

profile of v0, /device:TPU:0, one launch (start us, length us, event | category | flops | bytes accessed | tf_op | source)
XLA Modules:
  0.0 273.4 jit_solution(10275499087581960177)
XLA Ops:
  6.5 0.7 all-gather.7.cloned.1.call-update
  7.3 0.7 all-gather.9.cloned.1.call-update
  8.1 0.7 all-gather.5.cloned.1.call-update
  8.8 0.7 fusion.22
  9.4 1.1 reduce-window.6
  10.6 0.2 slice_reduce_fusion
  10.8 0.8 fusion.20
  11.7 0.7 dynamic-slice_bitcast_fusion
  12.4 1.9 gather_fusion
  14.3 1.9 gather_fusion.2
  16.2 0.7 fusion.21
  17.4 1.9 gather_fusion.1
  19.3 0.7 fusion.46
  20.6 0.7 fusion.47
  21.4 9.7 %fusion.41 = (f32[256]{0:T(256)S(1)}, s32[256]{0:T(256)S(1)}, s32[256]{0:T(256)S(1)}) fusion(s32[256]{0:T(256)S(1)} %gather_fusion.2, s32[]{:T(128)} %bitcast.19, s32[]{:T(128)} %bitcast.18, s32[]{:T(128)} %bitcast.17, s32[]{:T(128)} %bitcast.16, s32[]{:T(128)} %bitcast.15, s32[]{:T(128)} %bitcast.14, s32[]{:T(128)} %bitcast.13, s32[]{:T(128)} %bitcast.12, ...), kind=kLoop, calls=%fused_computation.94 | loop fusion | flops 15616 | bytes 6208 | tf_op jit(solution)/shard_map/convert_element_type | solution.py:22
  31.1 0.3 multiply_cosine_fusion
  31.4 29.8 %all-gather.7.cloned.1.call-done = bf16[8192,128]{1,0:T(8,128)(2,1)} async-done(((bf16[1024,128]{1,0:T(8,128)(2,1)}), bf16[8192,128]{1,0:T(8,128)(2,1)}) %all-gather.7.cloned.1.call-update) | async-done | bytes 2097168 | tf_op jit(solution)/shard_map/all_gather | solution.py:163
  61.3 4.4 %convolution_select_fusion = f32[256,128]{0,1:T(8,128)S(1)} fusion(bf16[256,8192]{1,0:T(8,128)(2,1)} %param.21, bf16[8192,128]{1,0:T(8,128)(2,1)} %all-gather.7.cloned.1.call-done, s32[256]{0:T(256)S(1)} %get-tuple-element.40, s32[128]{0:T(128)S(1)} %and_select_fusion.2), kind=kOutput, calls=%fused_computation.7 | convolution fusion | flops 536936448 | bytes 6424064 | tf_op jit(solution)/shard_map/dot_general | solution.py:164
  65.6 69.1 %all-gather.9.cloned.1.call-done = bf16[8192,256]{1,0:T(8,128)(2,1)} async-done(((bf16[1024,256]{1,0:T(8,128)(2,1)}), bf16[8192,256]{1,0:T(8,128)(2,1)}) %all-gather.9.cloned.1.call-update) | async-done | bytes 4194320 | tf_op jit(solution)/shard_map/all_gather | solution.py:162
  134.7 5.2 %fusion.51 = f32[256,256]{0,1:T(8,128)S(1)} fusion(bf16[256,8192]{1,0:T(8,128)(2,1)} %param.21, bf16[8192,256]{1,0:T(8,128)(2,1)} %all-gather.9.cloned.1.call-done), kind=kOutput, calls=%fused_computation.123 | convolution fusion | flops 1073741824 | bytes 8650752 | tf_op jit(solution)/shard_map/dot_general | solution.py:159
  139.9 0.3 fusion
  140.3 67.9 %all-gather.5.cloned.1.call-done = bf16[8192,256]{1,0:T(8,128)(2,1)} async-done(((bf16[1024,256]{1,0:T(8,128)(2,1)}), bf16[8192,256]{1,0:T(8,128)(2,1)}) %all-gather.5.cloned.1.call-update) | async-done | bytes 4194320 | tf_op jit(solution)/shard_map/all_gather | solution.py:161
  208.2 5.2 %fusion.50 = f32[256,256]{0,1:T(8,128)S(1)} fusion(bf16[256,8192]{1,0:T(8,128)(2,1)} %param.21, bf16[8192,256]{1,0:T(8,128)(2,1)} %all-gather.5.cloned.1.call-done), kind=kOutput, calls=%fused_computation.122 | convolution fusion | flops 1073741824 | bytes 8650752 | tf_op jit(solution)/shard_map/dot_general | solution.py:159
  213.5 0.3 convolution_add_fusion.1
  214.0 2.2 scatter_custom_fusion
  216.2 3.4 %all-to-all-start = ((bf16[8,32,512]{2,1,0:T(8,128)(2,1)}), bf16[8,32,512]{2,1,0:T(8,128)(2,1)S(1)}, u32[]{:S(2)}, u32[]{:S(2)}) async-start(bf16[8,32,512]{2,1,0:T(8,128)(2,1)} %bitcast.24), calls=%async_computation | async-start | bytes 524288 | tf_op jit(solution)/shard_map/all_to_all | solution.py:181
  220.0 0.2 fusion.48
  220.2 8.0 %all-to-all-done = bf16[8,32,512]{2,1,0:T(8,128)(2,1)S(1)} async-done(((bf16[8,32,512]{2,1,0:T(8,128)(2,1)}), bf16[8,32,512]{2,1,0:T(8,128)(2,1)S(1)}, u32[]{:S(2)}, u32[]{:S(2)}) %all-to-all-start) | async-done | bytes 262176 | tf_op jit(solution)/shard_map/all_to_all | solution.py:181
  228.3 0.2 fusion.49
  229.2 30.5 %all-gather = bf16[8,1,2048]{2,1,0:T(2,128)(2,1)S(1)} all-gather(bf16[1,1,2048]{2,1,0:T(2,128)(2,1)S(1)} %reshape.342), channel_id=1, replica_groups=mesh['group'=2,'dev'=8,'tp'=2] {'dev'}, dimensions={0}, use_global_device_ids=true | all-gather | bytes 36864 | tf_op jit(solution)/shard_map/all_gather | solution.py:199
  259.7 2.8 %fusion.16 = f32[8,1024]{1,0:T(8,128)S(1)} fusion(bf16[2048,1024]{1,0:T(8,128)(2,1)} %param.35, bf16[8,1,2048]{2,1,0:T(2,128)(2,1)S(1)} %all-gather), kind=kOutput, calls=%fused_computation.34 | convolution fusion | flops 33554432 | bytes 4259840 | tf_op jit(solution)/shard_map/dot_general | solution.py:200
  262.9 4.0 %psum.7 = bf16[8,1024]{1,0:T(8,128)(2,1)} all-reduce(f32[8,1024]{1,0:T(8,128)S(1)} %convolution_add_fusion.2), channel_id=1, replica_groups=mesh['group'=2,'dev'=8,'tp'=2] {'tp'}, use_global_device_ids=true, to_apply=%region_11.14 | all-reduce | flops 8192 | bytes 49152 | tf_op jit(solution)/shard_map/psum | solution.py:205
  (63 shorter events, 2.5 us)
Async XLA Ops:
  6.5 256.0 %copy-start = (bf16[2048,64]{0,1:T(8,128)(2,1)S(1)}, bf16[2048,64]{0,1:T(8,128)(2,1)}, u32[]{:S(2)}) copy-start(bf16[2048,64]{0,1:T(8,128)(2,1)} %param.36) | copy-start | bytes 786436
  6.5 12.8 %copy-start.4 = (s32[8]{0:T(128)S(1)}, s32[8]{0:T(128)}, u32[]{:S(2)}) copy-start(s32[8]{0:T(128)} %param.29) | copy-start | bytes 100
  6.5 14.1 %copy-start.6 = (s32[8]{0:T(128)S(1)}, s32[8]{0:T(128)}, u32[]{:S(2)}) copy-start(s32[8]{0:T(128)} %param.27) | copy-start | bytes 100
  6.5 54.7 %all-gather.7.cloned.1.call-start = ((), (), s32[]{:S(2)}) async-start(), calls=%async_computation.2 | async-start | bytes 2359296 | tf_op jit(solution)/shard_map/all_gather | solution.py:163
  7.3 127.5 %all-gather.9.cloned.1.call-start = ((), (), s32[]{:S(2)}) async-start(), calls=%async_computation.3 | async-start | bytes 4718592 | tf_op jit(solution)/shard_map/all_gather | solution.py:162
  8.0 200.2 %all-gather.5.cloned.1.call-start = ((), (), s32[]{:S(2)}) async-start(), calls=%async_computation.1 | async-start | bytes 4718592 | tf_op jit(solution)/shard_map/all_gather | solution.py:161
  65.6 74.3 %copy-start.7 = (bf16[64,256]{1,0:T(8,128)(2,1)S(1)}, bf16[64,256]{1,0:T(8,128)(2,1)}, u32[]{:S(2)}) copy-start(bf16[64,256]{1,0:T(8,128)(2,1)} %param.26) | copy-start | bytes 98308
  140.3 73.2 %copy-start.5 = (bf16[64,256]{1,0:T(8,128)(2,1)S(1)}, bf16[64,256]{1,0:T(8,128)(2,1)}, u32[]{:S(2)}) copy-start(bf16[64,256]{1,0:T(8,128)(2,1)} %param.25) | copy-start | bytes 98308
  140.3 79.3 %copy-start.9 = (bf16[1,256]{1,0:T(2,128)(2,1)S(1)}, bf16[1,256]{1,0:T(2,128)(2,1)}, u32[]{:S(2)}) copy-start(bf16[1,256]{1,0:T(2,128)(2,1)} %param.32) | copy-start | bytes 1540
  140.3 79.4 %copy-start.1 = (bf16[1,256,256]{2,1,0:T(8,128)(2,1)S(1)}, bf16[1,256,256]{2,1,0:T(8,128)(2,1)}, u32[]{:S(2)}) copy-start(bf16[1,256,256]{2,1,0:T(8,128)(2,1)} %param.33) | copy-start | bytes 393220
  140.3 79.5 %copy-start.2 = (bf16[1,256,256]{2,1,0:T(8,128)(2,1)S(1)}, bf16[1,256,256]{2,1,0:T(8,128)(2,1)}, u32[]{:S(2)}) copy-start(bf16[1,256,256]{2,1,0:T(8,128)(2,1)} %param.34) | copy-start | bytes 393220
  140.3 79.5 %copy-start.8 = (bf16[1,2048]{1,0:T(2,128)(2,1)S(1)}, bf16[1,2048]{1,0:T(2,128)(2,1)}, u32[]{:S(2)}) copy-start(bf16[1,2048]{1,0:T(2,128)(2,1)} %param.30) | copy-start | bytes 12292
  140.3 79.5 %copy-start.10 = (bf16[1,256]{1,0:T(2,128)(2,1)S(1)}, bf16[1,256]{1,0:T(2,128)(2,1)}, u32[]{:S(2)}) copy-start(bf16[1,256]{1,0:T(2,128)(2,1)} %param.31) | copy-start | bytes 1540
  213.9 48.9 %copy-start.3 = (bf16[64,1024]{1,0:T(8,128)(2,1)S(1)}, bf16[64,1024]{1,0:T(8,128)(2,1)}, u32[]{:S(2)}) copy-start(bf16[64,1024]{1,0:T(8,128)(2,1)} %param.37) | copy-start | bytes 393220
  216.2 12.0 %all-to-all-start = ((bf16[8,32,512]{2,1,0:T(8,128)(2,1)}), bf16[8,32,512]{2,1,0:T(8,128)(2,1)S(1)}, u32[]{:S(2)}, u32[]{:S(2)}) async-start(bf16[8,32,512]{2,1,0:T(8,128)(2,1)} %bitcast.24), calls=%async_computation | async-start | bytes 524288 | tf_op jit(solution)/shard_map/all_to_all | solution.py:181
Sparse Core Ops, SparseCore 0:
  9.5 51.7 all-gather.6
  63.4 71.3 all-gather.8
  136.9 71.3 all-gather.4
where the time goes:
time: 274 us; the launch traced here: 273 us
  waiting for transfers between devices  177 us (65%)
  blocking collectives  34.5 us (13%)
  matrix products  19.5 us (7%)
  other arithmetic  14.3 us (5%)
  between operations  14 us (5%)
  local copies, waits for them, and re-layouts  10.7 us (4%)
  starting transfers between devices  3.49 us (1%)
    all_gather x1, waiting for transfers between devices, per_device(): lax.all_gather(value_matrix, 'dev', axis=0, tiled=True)  69.1 us
    all_gather x1, waiting for transfers between devices, per_device(): key_raw = add_rows(lax.all_gather(key_matrix, 'dev', axis=0, tiled=True))  67.9 us
    all_gather x1, blocking collectives, per_device(): portion = lax.all_gather(mixed_local, 'dev', axis=0, tiled=True)  30.5 us
    all_gather x1, waiting for transfers between devices, per_device(): lax.all_gather(adapter_down_keyvalue, 'dev', axis=0, tiled=True)  29.8 us
    dot_general x2, matrix products, add_rows(): jnp.dot(prompt_activations, portion, preferred_element_type=jnp.float32)  10.4 us
    convert_element_type x1, other arithmetic, rotate(): angles = positions.astype(jnp.float32)[:, None] * frequency[None, :]  9.74 us
    all_to_all x1, waiting for transfers between devices, per_device(): lax.all_to_all(outgoing, 'dev', split_axis=0, concat_axis=0, tiled=True)  8 us
  transfers between devices with their start and end apart: 4, of which 4 were waited for; matrix products, arithmetic and copies ran while one was open for 12% of the time, Pallas kernels for 0%

commit v1 on v0

--- a/solution.py
+++ b/solution.py
@@ -1,3 +1,4 @@
+import functools
 import jax
 import jax.numpy as jnp
 from jax import lax
@@ -11,6 +12,15 @@
 PAGE = 4
 adapter_scale = 1.0
 rope_base = 500000.0
+
+
+def bring_block_up(field, out_dim):
+    return jnp.concatenate(
+        jax.lax.all_to_all(jnp.stack([field] * jax.lax.axis_size("dev")), "dev", 0, 0), axis=out_dim
+    )
+
+
+treat_frames_now = functools.partial(bring_block_up, out_dim=0)
 
 
 def rotate(key_rows, positions):
@@ -196,7 +206,7 @@
         step_key[0],
         step_value[0],
     ).reshape(1, -1)
-    portion = lax.all_gather(mixed_local, "dev", axis=0, tiled=True)
+    portion = treat_frames_now(mixed_local)
     plain_result = jnp.dot(portion, output_matrix, preferred_element_type=jnp.float32)
     selected_output = selected_narrow(portion, adapter_down_output, request_adapter)
     partial_output = plain_result + adapter_scale * jnp.dot(

time: 274 us -> 256 us (0.934)
  blocking collectives: 34.5 us -> 3.99 us
  waiting for transfers between devices: 177 us -> 184 us
  starting transfers between devices: 3.49 us -> 7.08 us
    all_gather x1 -> x0, blocking collectives: 30.5 us -> none  [per_device(): portion = lax.all_gather(mixed_local, 'dev', axis=0, tiled=True)]
    all_to_all x0 -> x1, waiting for transfers between devices: none -> 6.68 us  [bring_block_up(): jax.lax.all_to_all(jnp.stack([field] * jax.lax.axis_size('dev')), 'dev',...]
    all_to_all x0 -> x1, starting transfers between devices: none -> 3.59 us  [bring_block_up(): jax.lax.all_to_all(jnp.stack([field] * jax.lax.axis_size('dev')), 'dev',...]
  transfers between devices with their start and end apart: 4 -> 5, of which waited for: 4 -> 5; matrix products, arithmetic and copies ran while one was open for 12% -> 13% of each run, Pallas kernels for 0% -> 0%
where the time goes in v1:
time: 256 us; the launch traced here: 255 us
  waiting for transfers between devices  184 us (72%)
  matrix products  19.5 us (8%)
  other arithmetic  15.1 us (6%)
  between operations  14 us (5%)
  local copies, waits for them, and re-layouts  11.9 us (5%)
  starting transfers between devices  7.08 us (3%)
  blocking collectives  3.99 us (2%)
    all_gather x1, waiting for transfers between devices, per_device(): lax.all_gather(value_matrix, 'dev', axis=0, tiled=True)  69.1 us
    all_gather x1, waiting for transfers between devices, per_device(): key_raw = add_rows(lax.all_gather(key_matrix, 'dev', axis=0, tiled=True))  67.9 us
    all_gather x1, waiting for transfers between devices, per_device(): lax.all_gather(adapter_down_keyvalue, 'dev', axis=0, tiled=True)  29.8 us
    dot_general x2, matrix products, add_rows(): jnp.dot(prompt_activations, portion, preferred_element_type=jnp.float32)  10.4 us
    convert_element_type x1, other arithmetic, rotate(): angles = positions.astype(jnp.float32)[:, None] * frequency[None, :]  9.74 us
    all_to_all x1, waiting for transfers between devices, per_device(): lax.all_to_all(outgoing, 'dev', split_axis=0, concat_axis=0, tiled=True)  8 us
    all_to_all x1, waiting for transfers between devices, bring_block_up(): jax.lax.all_to_all(jnp.stack([field] * jax.lax.axis_size('dev')), 'dev',...  6.68 us
  transfers between devices with their start and end apart: 5, of which 5 were waited for; matrix products, arithmetic and copies ran while one was open for 13% of the time, Pallas kernels for 0%

profile of v1, /device:TPU:0, one launch (start us, length us, event | category | flops | bytes accessed | tf_op | source)
XLA Modules:
  0.0 255.2 jit_solution(1719473546504224651)
XLA Ops:
  6.5 0.7 all-gather.6.cloned.1.call-update
  7.3 0.7 all-gather.8.cloned.1.call-update
  8.1 0.7 all-gather.4.cloned.1.call-update
  8.8 0.7 fusion.23
  9.4 1.1 reduce-window.6
  10.8 0.8 fusion.21
  11.7 0.7 dynamic-slice_bitcast_fusion
  12.4 1.9 gather_fusion
  14.3 1.9 gather_fusion.2
  16.2 0.7 fusion.22
  17.4 1.9 gather_fusion.1
  19.3 0.7 fusion.47
  20.6 0.7 fusion.48
  21.4 9.7 %fusion.42 = (f32[256]{0:T(256)S(1)}, s32[256]{0:T(256)S(1)}, s32[256]{0:T(256)S(1)}) fusion(s32[256]{0:T(256)S(1)} %gather_fusion.2, s32[]{:T(128)} %bitcast.19, s32[]{:T(128)} %bitcast.18, s32[]{:T(128)} %bitcast.17, s32[]{:T(128)} %bitcast.16, s32[]{:T(128)} %bitcast.15, s32[]{:T(128)} %bitcast.14, s32[]{:T(128)} %bitcast.13, s32[]{:T(128)} %bitcast.12, ...), kind=kLoop, calls=%fused_computation.95 | loop fusion | flops 15616 | bytes 6208 | tf_op jit(solution)/shard_map/convert_element_type | solution.py:32
  31.4 29.8 %all-gather.6.cloned.1.call-done = bf16[8192,128]{1,0:T(8,128)(2,1)} async-done(((bf16[1024,128]{1,0:T(8,128)(2,1)}), bf16[8192,128]{1,0:T(8,128)(2,1)}) %all-gather.6.cloned.1.call-update) | async-done | bytes 2097168 | tf_op jit(solution)/shard_map/all_gather | solution.py:173
  61.3 4.4 %convolution_select_fusion = f32[256,128]{0,1:T(8,128)S(1)} fusion(bf16[256,8192]{1,0:T(8,128)(2,1)} %param.21, bf16[8192,128]{1,0:T(8,128)(2,1)} %all-gather.6.cloned.1.call-done, s32[256]{0:T(256)S(1)} %get-tuple-element.40, s32[128]{0:T(128)S(1)} %and_select_fusion.2), kind=kOutput, calls=%fused_computation.7 | convolution fusion | flops 536936448 | bytes 6424064 | tf_op jit(solution)/shard_map/dot_general | solution.py:174
  65.6 69.1 %all-gather.8.cloned.1.call-done = bf16[8192,256]{1,0:T(8,128)(2,1)} async-done(((bf16[1024,256]{1,0:T(8,128)(2,1)}), bf16[8192,256]{1,0:T(8,128)(2,1)}) %all-gather.8.cloned.1.call-update) | async-done | bytes 4194320 | tf_op jit(solution)/shard_map/all_gather | solution.py:172
  134.7 5.2 %fusion.52 = f32[256,256]{0,1:T(8,128)S(1)} fusion(bf16[256,8192]{1,0:T(8,128)(2,1)} %param.21, bf16[8192,256]{1,0:T(8,128)(2,1)} %all-gather.8.cloned.1.call-done), kind=kOutput, calls=%fused_computation.124 | convolution fusion | flops 1073741824 | bytes 8650752 | tf_op jit(solution)/shard_map/dot_general | solution.py:169
  139.9 0.3 fusion
  140.3 67.9 %all-gather.4.cloned.1.call-done = bf16[8192,256]{1,0:T(8,128)(2,1)} async-done(((bf16[1024,256]{1,0:T(8,128)(2,1)}), bf16[8192,256]{1,0:T(8,128)(2,1)}) %all-gather.4.cloned.1.call-update) | async-done | bytes 4194320 | tf_op jit(solution)/shard_map/all_gather | solution.py:171
  208.2 5.2 %fusion.51 = f32[256,256]{0,1:T(8,128)S(1)} fusion(bf16[256,8192]{1,0:T(8,128)(2,1)} %param.21, bf16[8192,256]{1,0:T(8,128)(2,1)} %all-gather.4.cloned.1.call-done), kind=kOutput, calls=%fused_computation.123 | convolution fusion | flops 1073741824 | bytes 8650752 | tf_op jit(solution)/shard_map/dot_general | solution.py:169
  213.5 0.3 convolution_add_fusion.1
  214.0 2.2 scatter_custom_fusion
  216.2 3.4 %all-to-all-start = ((bf16[8,32,512]{2,1,0:T(8,128)(2,1)}), bf16[8,32,512]{2,1,0:T(8,128)(2,1)S(1)}, u32[]{:S(2)}, u32[]{:S(2)}) async-start(bf16[8,32,512]{2,1,0:T(8,128)(2,1)} %bitcast.24), calls=%async_computation | async-start | bytes 524288 | tf_op jit(solution)/shard_map/all_to_all | solution.py:191
  220.2 8.0 %all-to-all-done = bf16[8,32,512]{2,1,0:T(8,128)(2,1)S(1)} async-done(((bf16[8,32,512]{2,1,0:T(8,128)(2,1)}), bf16[8,32,512]{2,1,0:T(8,128)(2,1)S(1)}, u32[]{:S(2)}, u32[]{:S(2)}) %all-to-all-start) | async-done | bytes 262176 | tf_op jit(solution)/shard_map/all_to_all | solution.py:191
  229.2 0.5 broadcast.390
  229.7 0.8 reduce.7
  230.5 0.6 reshape.379
  231.2 3.6 %all-to-all-start.1 = ((bf16[8,2,1024]{2,1,0:T(2,128)(2,1)}), bf16[8,2,1024]{2,1,0:T(2,128)(2,1)S(1)}, u32[]{:S(2)}, u32[]{:S(2)}) async-start(bf16[8,2,1024]{2,1,0:T(2,128)(2,1)} %reshape.379), calls=%async_computation.1 | async-start | bytes 65536 | tf_op jit(solution)/shard_map/all_to_all | solution.py:19
  234.8 6.7 %all-to-all-done.1 = bf16[8,2,1024]{2,1,0:T(2,128)(2,1)S(1)} async-done(((bf16[8,2,1024]{2,1,0:T(2,128)(2,1)}), bf16[8,2,1024]{2,1,0:T(2,128)(2,1)S(1)}, u32[]{:S(2)}, u32[]{:S(2)}) %all-to-all-start.1) | async-done | bytes 32800 | tf_op jit(solution)/shard_map/all_to_all | solution.py:19
  241.5 2.8 %fusion.17 = f32[8,1024]{1,0:T(8,128)S(1)} fusion(bf16[2048,1024]{1,0:T(8,128)(2,1)} %param.35, bf16[8,1,2048]{2,1,0:T(2,128)(2,1)S(1)} %reshape.380), kind=kOutput, calls=%fused_computation.35 | convolution fusion | flops 33554432 | bytes 4259840 | tf_op jit(solution)/shard_map/dot_general | solution.py:210
  244.7 4.0 %psum.7 = bf16[8,1024]{1,0:T(8,128)(2,1)} all-reduce(f32[8,1024]{1,0:T(8,128)S(1)} %convolution_add_fusion.2), channel_id=1, replica_groups=mesh['group'=2,'dev'=8,'tp'=2] {'tp'}, use_global_device_ids=true, to_apply=%region_11.14 | all-reduce | flops 8192 | bytes 49152 | tf_op jit(solution)/shard_map/psum | solution.py:215
  (68 shorter events, 3.6 us)
Async XLA Ops:
  6.5 237.8 %copy-start = (bf16[2048,64]{0,1:T(8,128)(2,1)S(1)}, bf16[2048,64]{0,1:T(8,128)(2,1)}, u32[]{:S(2)}) copy-start(bf16[2048,64]{0,1:T(8,128)(2,1)} %param.36) | copy-start | bytes 786436
  6.5 12.8 %copy-start.4 = (s32[8]{0:T(128)S(1)}, s32[8]{0:T(128)}, u32[]{:S(2)}) copy-start(s32[8]{0:T(128)} %param.29) | copy-start | bytes 100
  6.5 14.1 %copy-start.6 = (s32[8]{0:T(128)S(1)}, s32[8]{0:T(128)}, u32[]{:S(2)}) copy-start(s32[8]{0:T(128)} %param.27) | copy-start | bytes 100
  6.5 54.7 %all-gather.6.cloned.1.call-start = ((), (), s32[]{:S(2)}) async-start(), calls=%async_computation.3 | async-start | bytes 2359296 | tf_op jit(solution)/shard_map/all_gather | solution.py:173
  7.3 127.5 %all-gather.8.cloned.1.call-start = ((), (), s32[]{:S(2)}) async-start(), calls=%async_computation.4 | async-start | bytes 4718592 | tf_op jit(solution)/shard_map/all_gather | solution.py:172
  8.0 200.2 %all-gather.4.cloned.1.call-start = ((), (), s32[]{:S(2)}) async-start(), calls=%async_computation.2 | async-start | bytes 4718592 | tf_op jit(solution)/shard_map/all_gather | solution.py:171
  65.6 74.3 %copy-start.7 = (bf16[64,256]{1,0:T(8,128)(2,1)S(1)}, bf16[64,256]{1,0:T(8,128)(2,1)}, u32[]{:S(2)}) copy-start(bf16[64,256]{1,0:T(8,128)(2,1)} %param.26) | copy-start | bytes 98308
  140.3 73.2 %copy-start.5 = (bf16[64,256]{1,0:T(8,128)(2,1)S(1)}, bf16[64,256]{1,0:T(8,128)(2,1)}, u32[]{:S(2)}) copy-start(bf16[64,256]{1,0:T(8,128)(2,1)} %param.25) | copy-start | bytes 98308
  140.3 79.3 %copy-start.9 = (bf16[1,256]{1,0:T(2,128)(2,1)S(1)}, bf16[1,256]{1,0:T(2,128)(2,1)}, u32[]{:S(2)}) copy-start(bf16[1,256]{1,0:T(2,128)(2,1)} %param.32) | copy-start | bytes 1540
  140.3 79.4 %copy-start.1 = (bf16[1,256,256]{2,1,0:T(8,128)(2,1)S(1)}, bf16[1,256,256]{2,1,0:T(8,128)(2,1)}, u32[]{:S(2)}) copy-start(bf16[1,256,256]{2,1,0:T(8,128)(2,1)} %param.33) | copy-start | bytes 393220
  140.3 79.5 %copy-start.2 = (bf16[1,256,256]{2,1,0:T(8,128)(2,1)S(1)}, bf16[1,256,256]{2,1,0:T(8,128)(2,1)}, u32[]{:S(2)}) copy-start(bf16[1,256,256]{2,1,0:T(8,128)(2,1)} %param.34) | copy-start | bytes 393220
  140.3 79.5 %copy-start.8 = (bf16[1,2048]{1,0:T(2,128)(2,1)S(1)}, bf16[1,2048]{1,0:T(2,128)(2,1)}, u32[]{:S(2)}) copy-start(bf16[1,2048]{1,0:T(2,128)(2,1)} %param.30) | copy-start | bytes 12292
  140.3 79.5 %copy-start.10 = (bf16[1,256]{1,0:T(2,128)(2,1)S(1)}, bf16[1,256]{1,0:T(2,128)(2,1)}, u32[]{:S(2)}) copy-start(bf16[1,256]{1,0:T(2,128)(2,1)} %param.31) | copy-start | bytes 1540
  214.0 30.5 %copy-start.3 = (bf16[64,1024]{1,0:T(8,128)(2,1)S(1)}, bf16[64,1024]{1,0:T(8,128)(2,1)}, u32[]{:S(2)}) copy-start(bf16[64,1024]{1,0:T(8,128)(2,1)} %param.37) | copy-start | bytes 393220
  216.2 12.0 %all-to-all-start = ((bf16[8,32,512]{2,1,0:T(8,128)(2,1)}), bf16[8,32,512]{2,1,0:T(8,128)(2,1)S(1)}, u32[]{:S(2)}, u32[]{:S(2)}) async-start(bf16[8,32,512]{2,1,0:T(8,128)(2,1)} %bitcast.24), calls=%async_computation | async-start | bytes 524288 | tf_op jit(solution)/shard_map/all_to_all | solution.py:191
  231.2 10.3 %all-to-all-start.1 = ((bf16[8,2,1024]{2,1,0:T(2,128)(2,1)}), bf16[8,2,1024]{2,1,0:T(2,128)(2,1)S(1)}, u32[]{:S(2)}, u32[]{:S(2)}) async-start(bf16[8,2,1024]{2,1,0:T(2,128)(2,1)} %reshape.379), calls=%async_computation.1 | async-start | bytes 65536 | tf_op jit(solution)/shard_map/all_to_all | solution.py:19
Sparse Core Ops, SparseCore 0:
  9.5 51.7 all-gather.5
  63.4 71.3 all-gather.7
  136.9 71.3 all-gather.3
